TPU v7x, 512 devices: a whole 4x8x8 slice. The times are simulated.
512 devices in a mesh: dp: 8 (over y_hi, core), expert: 64 (over z, x, y_lo).
Axes of the slice: x: 4, y: 8 (y_hi: 4, y_lo: 2; y = y_hi * 2 + y_lo), z: 8, core: 2. Of those that a mesh axis runs over, the one named last changes fastest.
Arguments:
- tokens: bfloat16 [65536, 3584], P(('dp', 'expert')), may hold values from -6 to 6
- cotangent: bfloat16 [65536, 3584], P(('dp', 'expert')), may hold values from -0.59765625 to 0.59765625
- route_ids: int32 [65536, 8], P(('dp', 'expert')), may hold values from 0 to 383, as said below
- gates: bfloat16 [65536, 8], P(('dp', 'expert')), may hold values from 0.099609375 to 1
- w_gate: bfloat16 [64, 3584, 128], P('expert', None, 'dp'), may hold values from -0.09375 to 0.09375
- w_up: bfloat16 [64, 3584, 128], P('expert', None, 'dp'), may hold values from -0.09375 to 0.09375
- w_down: bfloat16 [64, 3584, 128], P('expert', None, 'dp'), may hold values from -0.125 to 0.125
Outputs:
- relaid_gate: bfloat16 [64, 3584, 128], P('expert', 'dp')
- relaid_up: bfloat16 [64, 3584, 128], P('expert', 'dp')
- relaid_down: bfloat16 [64, 3584, 128], P('expert', 'dp')
- grad_gate: float32 [64, 3584, 128], P('expert', 'dp')
- grad_up: float32 [64, 3584, 128], P('expert', 'dp')
- grad_down: float32 [64, 3584, 128], P('expert', 'dp')
- token_grad: bfloat16 [65536, 3584], P(('dp', 'expert'))
- gate_grad: float32 [65536, 8], P(('dp', 'expert'))
Inputs may be any that keep to these rules, and one draw needn't show every extreme that they name: `route_ids`: each row names 8 different experts. Among the 128 rows of one device, at most 6 routes name any one expert below 4; on every device of one index of dp, one same expert below 4 is named by exactly 6 routes.
All inputs are finite; a program needn't handle non-finite values.
Results may differ from a plain program's by a relative error of at most 0.02.
Values may be sent and summed in bfloat16 or wider, within the bound.
No kernel may reach another device: no remote copies, remote signals or barrier semaphores. Data moves between devices by JAX's collectives and lax.ppermute only.
A program may use at most 128 MiB of HBM per device.

v0:
```python
import jax
import jax.numpy as jnp
from jax import lax
from jax.sharding import PartitionSpec as P

HSPLIT = 16
CAP = 6


def copies(values, experts):
    grouped = values.reshape((experts, CAP) + values.shape[1:])
    return jnp.repeat(grouped, HSPLIT, axis=0)


def forward_part(slot_tokens, gate_slab, up_slab):
    pre_gate = jnp.dot(slot_tokens, gate_slab, preferred_element_type=jnp.float32)
    pre_up = jnp.dot(slot_tokens, up_slab, preferred_element_type=jnp.float32)
    sigmoid_gate = jax.nn.sigmoid(pre_gate)
    activation = pre_gate * sigmoid_gate
    hidden = (activation * pre_up).astype(jnp.bfloat16)
    return (pre_gate, pre_up, sigmoid_gate, activation, hidden)


def shards(tokens, cotangent, route_ids, gates, w_gate, w_up, w_down):
    slabs = lax.axis_size("expert")
    experts = slabs // HSPLIT
    tok_count, features = tokens.shape
    top_count = route_ids.shape[1]
    slot_total = experts * CAP
    flat_ids = route_ids.reshape(-1)
    expert_hits = (flat_ids[:, None] == jnp.arange(experts, dtype=jnp.int32)[None, :]).astype(
        jnp.int32
    )
    earlier = jnp.cumsum(expert_hits, axis=0) - expert_hits
    slot_rank = jnp.sum(earlier * expert_hits, axis=1)
    in_slab = jnp.sum(expert_hits, axis=1) > 0
    slot_index = flat_ids * CAP + slot_rank
    table = (slot_index[:, None] == jnp.arange(slot_total, dtype=jnp.int32)[None, :]) & in_slab[
        :, None
    ]
    select = table.reshape(tok_count, top_count, slot_total)
    picked = jnp.any(select, axis=1)
    pick_half = picked.astype(jnp.bfloat16)
    token_slots = jnp.einsum(
        "tc,td->cd", pick_half, tokens, preferred_element_type=jnp.float32
    ).astype(jnp.bfloat16)
    cotan_slots = jnp.einsum(
        "tc,td->cd", pick_half, cotangent, preferred_element_type=jnp.float32
    ).astype(jnp.bfloat16)
    gate_slots = jnp.sum(
        jnp.where(select, gates[:, :, None].astype(jnp.float32), 0.0), axis=(0, 1)
    ).astype(jnp.bfloat16)
    send_tok = copies(token_slots, experts)
    send_cotan = copies(cotan_slots, experts)
    send_gate = copies(gate_slots, experts)
    new_gate, new_up, new_down = (
        lax.all_to_all(w_gate, "dp", split_axis=1, concat_axis=2, tiled=True),
        lax.all_to_all(w_up, "dp", split_axis=1, concat_axis=2, tiled=True),
        lax.all_to_all(w_down, "dp", split_axis=1, concat_axis=2, tiled=True),
    )
    full_gate, full_up, full_down = (
        lax.all_gather(new_gate, "dp", axis=1, tiled=True),
        lax.all_gather(new_up, "dp", axis=1, tiled=True),
        lax.all_gather(new_down, "dp", axis=1, tiled=True),
    )
    gate_slab = full_gate[0]
    up_slab = full_up[0]
    down_slab = full_down[0]
    recv_tok, recv_cotan, recv_gate = (
        lax.all_to_all(send_tok, "expert", split_axis=0, concat_axis=0, tiled=True),
        lax.all_to_all(send_cotan, "expert", split_axis=0, concat_axis=0, tiled=True),
        lax.all_to_all(send_gate, "expert", split_axis=0, concat_axis=0, tiled=True),
    )
    slot_tokens = recv_tok.reshape(-1, features)
    pre_gate, pre_up, sigmoid_gate, activation, hidden = forward_part(
        slot_tokens, gate_slab, up_slab
    )
    slot_cotan = recv_cotan.reshape(-1, features)
    slot_gates = recv_gate.reshape(-1).astype(jnp.float32)[:, None]
    back_proj = jnp.dot(slot_cotan, down_slab, preferred_element_type=jnp.float32)
    score_part = jnp.sum(hidden.astype(jnp.float32) * back_proj, axis=1).astype(jnp.bfloat16)
    scaled = slot_gates * back_proj
    d_gate = (scaled * pre_up * sigmoid_gate * (1.0 + pre_gate * (1.0 - sigmoid_gate))).astype(
        jnp.bfloat16
    )
    d_up = (scaled * activation).astype(jnp.bfloat16)
    hidden_gated = (slot_gates * hidden.astype(jnp.float32)).astype(jnp.bfloat16)
    partial_value = (
        jnp.einsum("rh,dh->rd", d_gate, gate_slab, preferred_element_type=jnp.float32)
        + jnp.einsum("rh,dh->rd", d_up, up_slab, preferred_element_type=jnp.float32)
    ).astype(jnp.bfloat16)
    grad_gate_part = jnp.einsum(
        "rd,rh->dh", slot_tokens, d_gate, preferred_element_type=jnp.float32
    )
    grad_up_part = jnp.einsum("rd,rh->dh", slot_tokens, d_up, preferred_element_type=jnp.float32)
    grad_down_part = jnp.einsum(
        "rd,rh->dh", slot_cotan, hidden_gated, preferred_element_type=jnp.float32
    )
    grad_gate, grad_up, grad_down = (
        lax.psum_scatter(
            grad_gate_part[None].astype(jnp.bfloat16), "dp", scatter_dimension=1, tiled=True
        ).astype(jnp.float32),
        lax.psum_scatter(
            grad_up_part[None].astype(jnp.bfloat16), "dp", scatter_dimension=1, tiled=True
        ).astype(jnp.float32),
        lax.psum_scatter(
            grad_down_part[None].astype(jnp.bfloat16), "dp", scatter_dimension=1, tiled=True
        ).astype(jnp.float32),
    )
    back_parts, back_scores = (
        lax.all_to_all(
            partial_value.reshape(slabs, CAP, features),
            "expert",
            split_axis=0,
            concat_axis=0,
            tiled=True,
        ),
        lax.all_to_all(
            score_part.reshape(slabs, CAP), "expert", split_axis=0, concat_axis=0, tiled=True
        ),
    )
    part_sum = jnp.sum(
        back_parts.reshape(experts, HSPLIT, CAP, features).astype(jnp.float32), axis=1
    )
    part_sum = part_sum.reshape(slot_total, features)
    score_sum = jnp.sum(
        back_scores.reshape(experts, HSPLIT, CAP).astype(jnp.float32), axis=1
    ).reshape(slot_total)
    token_grad = jnp.einsum(
        "tc,cd->td", picked.astype(jnp.float32), part_sum, precision=lax.Precision.HIGHEST
    ).astype(jnp.bfloat16)
    gate_grad = jnp.einsum(
        "tkc,c->tk", select.astype(jnp.float32), score_sum, precision=lax.Precision.HIGHEST
    )
    return (new_gate, new_up, new_down, grad_gate, grad_up, grad_down, token_grad, gate_grad)


def solution(mesh):
    in_specs = (
        P(("dp", "expert"), None),
        P(("dp", "expert"), None),
        P(("dp", "expert"), None),
        P(("dp", "expert"), None),
        P("expert", None, "dp"),
        P("expert", None, "dp"),
        P("expert", None, "dp"),
    )
    out_specs = (
        P("expert", "dp", None),
        P("expert", "dp", None),
        P("expert", "dp", None),
        P("expert", "dp", None),
        P("expert", "dp", None),
        P("expert", "dp", None),
        P(("dp", "expert"), None),
        P(("dp", "expert"), None),
    )
    return jax.shard_map(shards, mesh=mesh, in_specs=in_specs, out_specs=out_specs, check_vma=False)
```

profile of v0, /device:TPU:17, one launch (start us, length us, event | category | flops | bytes accessed | tf_op | source)
XLA Modules:
  0.0 506.8 jit_solution(7459007044376049819)
XLA Ops:
  7.2 0.9 copy.114
  8.2 1.1 reduce-window.6
  9.4 0.2 slice_reduce_fusion
  9.6 0.2 reduce-window.9
  10.0 0.7 multiply_add_fusion
  10.9 0.7 convert_element_type.118
  12.1 0.7 copy.119
  12.9 14.5 %all-to-all-start.4 = ((bf16[64,1,6]{2,1,0:T(2,128)(2,1)}), bf16[64,1,6]{2,1,0:T(2,128)(2,1)S(1)}, u32[]{:S(2)}, u32[]{:S(2)}) async-start(bf16[64,1,6]{2,1,0:T(2,128)(2,1)} %copy.119), calls=%async_computation.4 | async-start | bytes 65536 | tf_op jit(solution)/shard_map/all_to_all | solution.py:72
  27.4 3.7 copy.105
  31.2 0.5 broadcast.78
  31.7 20.6 %reduce.6 = bf16[3584,16]{1,0:T(8,128)(2,1)} reduce(bf16[3584,1,16]{2,1,0:T(2,128)(2,1)S(1)} %bitcast.87, bf16[]{:T(256)} %broadcast.78), dimensions={1}, to_apply=%bitcast.58.reduce_sub_computation | reduce | bytes 229378
  52.3 2.8 reshape.176
  55.1 7.4 %all-to-all-start = ((bf16[8,2,3584]{2,1,0:T(2,128)(2,1)}), bf16[8,2,3584]{2,1,0:T(2,128)(2,1)S(1)}, u32[]{:S(2)}, u32[]{:S(2)}) async-start(bf16[8,2,3584]{2,1,0:T(2,128)(2,1)} %reshape.176), calls=%async_computation | async-start | bytes 229376 | tf_op jit(solution)/shard_map/all_to_all | solution.py:57
  62.6 2.5 copy.108
  65.0 20.6 %reduce.7 = bf16[3584,16]{1,0:T(8,128)(2,1)} reduce(bf16[3584,1,16]{2,1,0:T(2,128)(2,1)S(1)} %bitcast.92, bf16[]{:T(256)} %broadcast.78), dimensions={1}, to_apply=%bitcast.60.reduce_sub_computation | reduce | bytes 229378
  85.6 2.8 reshape.178
  88.4 7.8 %all-to-all-start.1 = ((bf16[8,2,3584]{2,1,0:T(2,128)(2,1)}), bf16[8,2,3584]{2,1,0:T(2,128)(2,1)S(1)}, u32[]{:S(2)}, u32[]{:S(2)}) async-start(bf16[8,2,3584]{2,1,0:T(2,128)(2,1)} %reshape.178), calls=%async_computation.1 | async-start | bytes 229376 | tf_op jit(solution)/shard_map/all_to_all | solution.py:58
  96.2 2.5 copy.111
  98.7 20.6 %reduce.8 = bf16[3584,16]{1,0:T(8,128)(2,1)} reduce(bf16[3584,1,16]{2,1,0:T(2,128)(2,1)S(1)} %bitcast.88, bf16[]{:T(256)} %broadcast.78), dimensions={1}, to_apply=%bitcast.62.reduce_sub_computation | reduce | bytes 229378
  119.3 2.8 reshape.180
  122.1 7.2 %all-to-all-start.2 = ((bf16[8,2,3584]{2,1,0:T(2,128)(2,1)}), bf16[8,2,3584]{2,1,0:T(2,128)(2,1)S(1)}, u32[]{:S(2)}, u32[]{:S(2)}) async-start(bf16[8,2,3584]{2,1,0:T(2,128)(2,1)} %reshape.180), calls=%async_computation.2 | async-start | bytes 229376 | tf_op jit(solution)/shard_map/all_to_all | solution.py:59
  129.3 0.2 convolution_convert_fusion.5
  129.6 5.3 %all-to-all-done.2 = bf16[8,2,3584]{2,1,0:T(2,128)(2,1)S(1)} async-done(((bf16[8,2,3584]{2,1,0:T(2,128)(2,1)}), bf16[8,2,3584]{2,1,0:T(2,128)(2,1)S(1)}, u32[]{:S(2)}, u32[]{:S(2)}) %all-to-all-start.2) | async-done | bytes 114720 | tf_op jit(solution)/shard_map/all_to_all | solution.py:59
  134.9 2.1 broadcast_in_dim.18
  137.0 11.7 %all-to-all-start.3 = ((bf16[64,6,3584]{2,1,0:T(8,128)(2,1)}), bf16[64,6,3584]{2,1,0:T(8,128)(2,1)}, u32[]{:S(2)}, u32[]{:S(2)}) async-start(bf16[64,6,3584]{2,1,0:T(8,128)(2,1)} %bitcast.86), calls=%async_computation.3 | async-start | bytes 7340032 | tf_op jit(solution)/shard_map/all_to_all | solution.py:70
  148.7 0.2 convolution_convert_fusion.4
  149.0 82.7 %all-to-all-done.3 = bf16[64,6,3584]{2,1,0:T(8,128)(2,1)} async-done(((bf16[64,6,3584]{2,1,0:T(8,128)(2,1)}), bf16[64,6,3584]{2,1,0:T(8,128)(2,1)}, u32[]{:S(2)}, u32[]{:S(2)}) %all-to-all-start.3) | async-done | bytes 2752544 | tf_op jit(solution)/shard_map/all_to_all | solution.py:70
  231.7 2.1 broadcast_in_dim.34
  233.9 8.0 %all-to-all-start.5 = ((bf16[64,6,3584]{2,1,0:T(8,128)(2,1)}), bf16[64,6,3584]{2,1,0:T(8,128)(2,1)}, u32[]{:S(2)}, u32[]{:S(2)}) async-start(bf16[64,6,3584]{2,1,0:T(8,128)(2,1)} %bitcast.85), calls=%async_computation.5 | async-start | bytes 7340032 | tf_op jit(solution)/shard_map/all_to_all | solution.py:71
  242.1 1.4 reshape.177
  243.5 1.8 copy.106
  245.3 0.2 all_to_all.59
  245.7 1.4 reshape.179
  247.1 1.8 copy.109
  248.9 0.2 all_to_all.63
  249.3 1.4 reshape.181
  250.7 1.8 copy.112
  252.9 47.2 %all_gather.10 = bf16[1,3584,128]{2,1,0:T(8,128)(2,1)S(1)} all-gather(bf16[1,448,128]{2,1,0:T(8,128)(2,1)S(1)} %copy.126), channel_id=1, replica_groups=mesh['dp'=8,'expert'=64] {'dp'}, dimensions={1}, use_global_device_ids=true | all-gather | bytes 1032192 | tf_op jit(solution)/shard_map/all_gather | solution.py:63
  300.0 16.3 %all_gather.11 = bf16[1,3584,128]{2,1,0:T(8,128)(2,1)S(1)} all-gather(bf16[1,448,128]{2,1,0:T(8,128)(2,1)S(1)} %copy.125), channel_id=1, replica_groups=mesh['dp'=8,'expert'=64] {'dp'}, dimensions={1}, use_global_device_ids=true | all-gather | bytes 1032192 | tf_op jit(solution)/shard_map/all_gather | solution.py:62
  316.4 16.9 %all_gather.9 = bf16[1,3584,128]{2,1,0:T(8,128)(2,1)} all-gather(bf16[1,448,128]{2,1,0:T(8,128)(2,1)S(1)} %copy.127), channel_id=1, replica_groups=mesh['dp'=8,'expert'=64] {'dp'}, dimensions={1}, use_global_device_ids=true | all-gather | bytes 1032192 | tf_op jit(solution)/shard_map/all_gather | solution.py:64
  333.3 5.5 %reshape.155 = bf16[384,3584]{1,0:T(8,128)(2,1)} reshape(bf16[64,6,3584]{2,1,0:T(8,128)(2,1)} %all-to-all-done.3) | data formatting | bytes 5505024 | tf_op jit(solution)/shard_map/reshape | solution.py:74
  338.8 2.9 fusion.9
  341.6 0.9 fusion.6
  342.6 5.5 %reshape.158 = bf16[384,3584]{1,0:T(8,128)(2,1)} reshape(bf16[64,6,3584]{2,1,0:T(8,128)(2,1)} %all-to-all-done.5) | data formatting | bytes 5505024 | tf_op jit(solution)/shard_map/reshape | solution.py:78
  348.1 3.1 fusion.14
  351.2 1.8 fusion.1
  353.1 3.3 fusion.4
  356.4 0.8 convert_element_type.149
  357.2 16.3 %all-to-all-start.7 = ((bf16[64,1,6]{2,1,0:T(2,128)(2,1)}), bf16[64,1,6]{2,1,0:T(2,128)(2,1)S(1)}, u32[]{:S(2)}, u32[]{:S(2)}) async-start(bf16[64,1,6]{2,1,0:T(2,128)(2,1)} %convert_element_type.149), calls=%async_computation.10 | async-start | bytes 65536 | tf_op jit(solution)/shard_map/all_to_all | solution.py:118
  373.4 5.1 fusion
  378.5 5.5 %reshape.159 = bf16[64,6,3584]{2,1,0:T(8,128)(2,1)} reshape(bf16[384,3584]{1,0:T(8,128)(2,1)} %fusion) | data formatting | bytes 5505024 | tf_op jit(solution)/shard_map/reshape | solution.py:112
  383.9 10.8 %all-to-all-start.6 = ((bf16[64,6,3584]{2,1,0:T(8,128)(2,1)}), bf16[64,6,3584]{2,1,0:T(8,128)(2,1)}, u32[]{:S(2)}, u32[]{:S(2)}) async-start(bf16[64,6,3584]{2,1,0:T(8,128)(2,1)} %reshape.159), calls=%async_computation.9 | async-start | bytes 7340032 | tf_op jit(solution)/shard_map/all_to_all | solution.py:111
  394.8 3.7 fusion.2
  398.5 0.3 reduce-scatter.8.cloned.1.call-start
  398.8 3.6 fusion.3
  402.6 0.7 fusion.23
  403.3 0.6 reduce-scatter.4.cloned.1.call-done
  403.9 1.6 convert_element_type.127
  405.5 44.8 %reduce-scatter.6.cloned.1.call-done = bf16[1,448,128]{2,1,0:T(8,128)(2,1)} async-done(((bf16[1,3584,128]{2,1,0:T(8,128)(2,1)}), bf16[1,448,128]{2,1,0:T(8,128)(2,1)}) %reduce-scatter.6.cloned.1.call-update) | async-done | bytes 114704 | tf_op jit(solution)/shard_map/reduce_scatter | solution.py:103
  450.3 1.6 convert_element_type.131
  451.9 41.8 %reduce-scatter.8.cloned.1.call-done = bf16[1,448,128]{2,1,0:T(8,128)(2,1)} async-done(((bf16[1,3584,128]{2,1,0:T(8,128)(2,1)}), bf16[1,448,128]{2,1,0:T(8,128)(2,1)}) %reduce-scatter.8.cloned.1.call-update) | async-done | bytes 114704 | tf_op jit(solution)/shard_map/reduce_scatter | solution.py:106
  493.7 1.6 convert_element_type.137
  495.4 2.8 convert_reduce_fusion
  498.2 1.8 convolution_convert_fusion
  (60 shorter events, 2.6 us)
Async XLA Ops:
  7.2 122.1 %copy-start = (bf16[128,3584]{1,0:T(8,128)(2,1)S(1)}, bf16[128,3584]{1,0:T(8,128)(2,1)}, u32[]{:S(2)}) copy-start(bf16[128,3584]{1,0:T(8,128)(2,1)} %param.7) | copy-start | bytes 2752516
  12.9 42.2 %all-to-all-start.4 = ((bf16[64,1,6]{2,1,0:T(2,128)(2,1)}), bf16[64,1,6]{2,1,0:T(2,128)(2,1)S(1)}, u32[]{:S(2)}, u32[]{:S(2)}) async-start(bf16[64,1,6]{2,1,0:T(2,128)(2,1)} %copy.119), calls=%async_computation.4 | async-start | bytes 65536 | tf_op jit(solution)/shard_map/all_to_all | solution.py:72
  27.4 35.1 %copy-start.7 = (bf16[1,3584,16]{1,2,0:T(8,128)(2,1)S(1)}, bf16[1,3584,16]{1,2,0:T(8,128)(2,1)}, u32[]{:S(2)}) copy-start(bf16[1,3584,16]{1,2,0:T(8,128)(2,1)} %param.12) | copy-start | bytes 344068
  55.1 33.3 %all-to-all-start = ((bf16[8,2,3584]{2,1,0:T(2,128)(2,1)}), bf16[8,2,3584]{2,1,0:T(2,128)(2,1)S(1)}, u32[]{:S(2)}, u32[]{:S(2)}) async-start(bf16[8,2,3584]{2,1,0:T(2,128)(2,1)} %reshape.176), calls=%async_computation | async-start | bytes 229376 | tf_op jit(solution)/shard_map/all_to_all | solution.py:57
  62.5 33.6 %copy-start.8 = (bf16[1,3584,16]{1,2,0:T(8,128)(2,1)S(1)}, bf16[1,3584,16]{1,2,0:T(8,128)(2,1)}, u32[]{:S(2)}) copy-start(bf16[1,3584,16]{1,2,0:T(8,128)(2,1)} %param.13) | copy-start | bytes 344068
  88.4 33.7 %all-to-all-start.1 = ((bf16[8,2,3584]{2,1,0:T(2,128)(2,1)}), bf16[8,2,3584]{2,1,0:T(2,128)(2,1)S(1)}, u32[]{:S(2)}, u32[]{:S(2)}) async-start(bf16[8,2,3584]{2,1,0:T(2,128)(2,1)} %reshape.178), calls=%async_computation.1 | async-start | bytes 229376 | tf_op jit(solution)/shard_map/all_to_all | solution.py:58
  122.1 12.8 %all-to-all-start.2 = ((bf16[8,2,3584]{2,1,0:T(2,128)(2,1)}), bf16[8,2,3584]{2,1,0:T(2,128)(2,1)S(1)}, u32[]{:S(2)}, u32[]{:S(2)}) async-start(bf16[8,2,3584]{2,1,0:T(2,128)(2,1)} %reshape.180), calls=%async_computation.2 | async-start | bytes 229376 | tf_op jit(solution)/shard_map/all_to_all | solution.py:59
  137.0 11.7 %copy-start.3 = (bf16[128,3584]{1,0:T(8,128)(2,1)S(1)}, bf16[128,3584]{1,0:T(8,128)(2,1)}, u32[]{:S(2)}) copy-start(bf16[128,3584]{1,0:T(8,128)(2,1)} %param.8) | copy-start | bytes 2752516
  137.0 94.7 %all-to-all-start.3 = ((bf16[64,6,3584]{2,1,0:T(8,128)(2,1)}), bf16[64,6,3584]{2,1,0:T(8,128)(2,1)}, u32[]{:S(2)}, u32[]{:S(2)}) async-start(bf16[64,6,3584]{2,1,0:T(8,128)(2,1)} %bitcast.86), calls=%async_computation.3 | async-start | bytes 7340032 | tf_op jit(solution)/shard_map/all_to_all | solution.py:70
  233.9 108.7 %all-to-all-start.5 = ((bf16[64,6,3584]{2,1,0:T(8,128)(2,1)}), bf16[64,6,3584]{2,1,0:T(8,128)(2,1)}, u32[]{:S(2)}, u32[]{:S(2)}) async-start(bf16[64,6,3584]{2,1,0:T(8,128)(2,1)} %bitcast.85), calls=%async_computation.5 | async-start | bytes 7340032 | tf_op jit(solution)/shard_map/all_to_all | solution.py:71
  241.9 162.1 %reduce-scatter.4.cloned.1.call-start = ((), (), s32[]{:S(2)}) async-start(), calls=%async_computation.11 | async-start | bytes 1032192 | tf_op jit(solution)/shard_map/reduce_scatter | solution.py:100
  245.7 54.3 %copy-start.4 = (bf16[1,448,128]{2,1,0:T(8,128)(2,1)}, bf16[1,448,128]{2,1,0:T(8,128)(2,1)S(1)}, u32[]{:S(2)}) copy-start(bf16[1,448,128]{2,1,0:T(8,128)(2,1)S(1)} %copy.125) | copy-start | bytes 344068
  249.3 50.8 %copy-start.5 = (bf16[1,448,128]{2,1,0:T(8,128)(2,1)}, bf16[1,448,128]{2,1,0:T(8,128)(2,1)S(1)}, u32[]{:S(2)}) copy-start(bf16[1,448,128]{2,1,0:T(8,128)(2,1)S(1)} %copy.126) | copy-start | bytes 344068
  252.9 85.9 %copy-start.6 = (bf16[1,448,128]{2,1,0:T(8,128)(2,1)}, bf16[1,448,128]{2,1,0:T(8,128)(2,1)S(1)}, u32[]{:S(2)}) copy-start(bf16[1,448,128]{2,1,0:T(8,128)(2,1)S(1)} %copy.127) | copy-start | bytes 344068
  338.8 2.9 copy-start.1
  348.1 3.1 copy-start.2
  357.2 26.8 %all-to-all-start.7 = ((bf16[64,1,6]{2,1,0:T(2,128)(2,1)}), bf16[64,1,6]{2,1,0:T(2,128)(2,1)S(1)}, u32[]{:S(2)}, u32[]{:S(2)}) async-start(bf16[64,1,6]{2,1,0:T(2,128)(2,1)} %convert_element_type.149), calls=%async_computation.10 | async-start | bytes 65536 | tf_op jit(solution)/shard_map/all_to_all | solution.py:118
  383.9 111.4 %all-to-all-start.6 = ((bf16[64,6,3584]{2,1,0:T(8,128)(2,1)}), bf16[64,6,3584]{2,1,0:T(8,128)(2,1)}, u32[]{:S(2)}, u32[]{:S(2)}) async-start(bf16[64,6,3584]{2,1,0:T(8,128)(2,1)} %reshape.159), calls=%async_computation.9 | async-start | bytes 7340032 | tf_op jit(solution)/shard_map/all_to_all | solution.py:111
  394.7 55.5 %reduce-scatter.6.cloned.1.call-start = ((), (), s32[]{:S(2)}) async-start(), calls=%async_computation.12 | async-start | bytes 1032192 | tf_op jit(solution)/shard_map/reduce_scatter | solution.py:103
  398.5 95.2 %reduce-scatter.8.cloned.1.call-start = ((), (), s32[]{:S(2)}) async-start(), calls=%async_computation.13 | async-start | bytes 1032192 | tf_op jit(solution)/shard_map/reduce_scatter | solution.py:106
Sparse Core Ops, SparseCore 0:
  356.5 47.3 reduce-scatter.3
  407.0 43.2 reduce-scatter.5
  453.1 40.5 reduce-scatter.7
where the time goes:
time: 514 us; the launch traced here: 507 us
  waiting for transfers between devices  175 us (34%)
  starting transfers between devices  84 us (16%)
  blocking collectives  80.4 us (16%)
  other arithmetic  72.6 us (14%)
  local copies, waits for them, and re-layouts  52.7 us (10%)
  matrix products  27.4 us (5%)
  between operations  14.4 us (3%)
    all_to_all x1, waiting for transfers between devices, shards(): lax.all_to_all(send_tok, 'expert', split_axis=0, concat_axis=0, tiled=True)  82.7 us
    unnamed x4, other arithmetic  61.9 us
    all_gather x1, blocking collectives, shards(): lax.all_gather(new_up, 'dp', axis=1, tiled=True)  47.2 us
    reduce_scatter x1, waiting for transfers between devices, shards(): lax.psum_scatter(grad_up_part[None].astype(jnp.bfloat16), 'dp', scatter_d...  44.8 us
    reduce_scatter x1, waiting for transfers between devices, shards(): lax.psum_scatter(grad_down_part[None].astype(jnp.bfloat16), 'dp', scatter...  41.8 us
    unnamed x32, local copies, waits for them, and re-layouts  23 us
    all_gather x1, blocking collectives, shards(): lax.all_gather(new_down, 'dp', axis=1, tiled=True)  16.9 us
    all_gather x1, blocking collectives, shards(): lax.all_gather(new_gate, 'dp', axis=1, tiled=True)  16.3 us
  transfers between devices with their start and end apart: 11, of which 5 were waited for; matrix products, arithmetic and copies ran while one was open for 24% of the time, Pallas kernels for 0%

commit v1 on v0

--- a/solution.py
+++ b/solution.py
@@ -58,10 +58,17 @@
         lax.all_to_all(w_up, "dp", split_axis=1, concat_axis=2, tiled=True),
         lax.all_to_all(w_down, "dp", split_axis=1, concat_axis=2, tiled=True),
     )
+
+    def find_the_rates(page):
+        seen = []
+        for _ in range(lax.axis_size("dp")):
+            seen.append(page)
+        return jnp.concatenate(lax.all_to_all(jnp.stack(seen, axis=0), "dp", 0, 0), 1)
+
     full_gate, full_up, full_down = (
         lax.all_gather(new_gate, "dp", axis=1, tiled=True),
         lax.all_gather(new_up, "dp", axis=1, tiled=True),
-        lax.all_gather(new_down, "dp", axis=1, tiled=True),
+        find_the_rates(new_down),
     )
     gate_slab = full_gate[0]
     up_slab = full_up[0]

time: 514 us -> 561 us (1.091)
  the two profiles are of different devices: /device:TPU:17 before, /device:TPU:23 now
where the time goes in v1:
time: 561 us; the launch traced here: 553 us
  waiting for transfers between devices  254 us (45%)
  starting transfers between devices  84.3 us (15%)
  other arithmetic  72.6 us (13%)
  local copies, waits for them, and re-layouts  54.5 us (10%)
  blocking collectives  45.4 us (8%)
  matrix products  28 us (5%)
  between operations  14.4 us (3%)
    all_to_all x1, waiting for transfers between devices, shards(): lax.all_to_all(send_tok, 'expert', split_axis=0, concat_axis=0, tiled=True)  83.3 us
    all_to_all x1, waiting for transfers between devices, shards(): lax.all_to_all(send_cotan, 'expert', split_axis=0, concat_axis=0, tiled=T...  79.2 us
    unnamed x4, other arithmetic  61.9 us
    reduce_scatter x1, waiting for transfers between devices, shards(): lax.psum_scatter(grad_up_part[None].astype(jnp.bfloat16), 'dp', scatter_d...  44.4 us
    reduce_scatter x1, waiting for transfers between devices, shards(): lax.psum_scatter(grad_down_part[None].astype(jnp.bfloat16), 'dp', scatter...  41.5 us
    all_gather x1, blocking collectives, shards(): lax.all_gather(new_up, 'dp', axis=1, tiled=True)  28.9 us
    unnamed x32, local copies, waits for them, and re-layouts  23.6 us
    all_gather x1, blocking collectives, shards(): lax.all_gather(new_gate, 'dp', axis=1, tiled=True)  16.6 us
  transfers between devices with their start and end apart: 12, of which 5 were waited for; matrix products, arithmetic and copies ran while one was open for 24% of the time, Pallas kernels for 0%

profile of v1, /device:TPU:23, one launch (start us, length us, event | category | flops | bytes accessed | tf_op | source)
XLA Modules:
  0.0 553.0 jit_solution(3049701806953665745)
XLA Ops:
  7.2 0.9 copy.117
  8.2 1.1 reduce-window.6
  9.4 0.2 slice_reduce_fusion
  9.6 0.2 reduce-window.9
  10.0 0.7 multiply_add_fusion
  10.9 0.7 convert_element_type.118
  12.1 0.7 copy.122
  12.9 14.3 %all-to-all-start.4 = ((bf16[64,1,6]{2,1,0:T(2,128)(2,1)}), bf16[64,1,6]{2,1,0:T(2,128)(2,1)S(1)}, u32[]{:S(2)}, u32[]{:S(2)}) async-start(bf16[64,1,6]{2,1,0:T(2,128)(2,1)} %copy.122), calls=%async_computation.4 | async-start | bytes 65536 | tf_op jit(solution)/shard_map/all_to_all | solution.py:79
  27.2 3.7 copy.108
  30.9 0.5 broadcast.80
  31.4 20.6 %reduce.6 = bf16[3584,16]{1,0:T(8,128)(2,1)} reduce(bf16[3584,1,16]{2,1,0:T(2,128)(2,1)S(1)} %bitcast.85, bf16[]{:T(256)} %broadcast.80), dimensions={1}, to_apply=%bitcast.57.reduce_sub_computation | reduce | bytes 229378
  52.0 2.8 reshape.181
  54.8 7.7 %all-to-all-start = ((bf16[8,2,3584]{2,1,0:T(2,128)(2,1)}), bf16[8,2,3584]{2,1,0:T(2,128)(2,1)S(1)}, u32[]{:S(2)}, u32[]{:S(2)}) async-start(bf16[8,2,3584]{2,1,0:T(2,128)(2,1)} %reshape.181), calls=%async_computation | async-start | bytes 229376 | tf_op jit(solution)/shard_map/all_to_all | solution.py:57
  62.6 2.5 copy.111
  65.0 20.6 %reduce.7 = bf16[3584,16]{1,0:T(8,128)(2,1)} reduce(bf16[3584,1,16]{2,1,0:T(2,128)(2,1)S(1)} %bitcast.90, bf16[]{:T(256)} %broadcast.80), dimensions={1}, to_apply=%bitcast.59.reduce_sub_computation | reduce | bytes 229378
  85.7 2.8 reshape.183
  88.4 7.8 %all-to-all-start.1 = ((bf16[8,2,3584]{2,1,0:T(2,128)(2,1)}), bf16[8,2,3584]{2,1,0:T(2,128)(2,1)S(1)}, u32[]{:S(2)}, u32[]{:S(2)}) async-start(bf16[8,2,3584]{2,1,0:T(2,128)(2,1)} %reshape.183), calls=%async_computation.1 | async-start | bytes 229376 | tf_op jit(solution)/shard_map/all_to_all | solution.py:58
  96.2 2.5 copy.114
  98.7 20.6 %reduce.8 = bf16[3584,16]{1,0:T(8,128)(2,1)} reduce(bf16[3584,1,16]{2,1,0:T(2,128)(2,1)S(1)} %bitcast.86, bf16[]{:T(256)} %broadcast.80), dimensions={1}, to_apply=%bitcast.61.reduce_sub_computation | reduce | bytes 229378
  119.3 2.8 reshape.185
  122.1 7.2 %all-to-all-start.2 = ((bf16[8,2,3584]{2,1,0:T(2,128)(2,1)}), bf16[8,2,3584]{2,1,0:T(2,128)(2,1)S(1)}, u32[]{:S(2)}, u32[]{:S(2)}) async-start(bf16[8,2,3584]{2,1,0:T(2,128)(2,1)} %reshape.185), calls=%async_computation.2 | async-start | bytes 229376 | tf_op jit(solution)/shard_map/all_to_all | solution.py:59
  129.3 0.2 convolution_convert_fusion.5
  129.6 5.3 all-to-all-done.2
  135.0 2.1 broadcast_in_dim.18
  137.0 11.4 %all-to-all-start.3 = ((bf16[64,6,3584]{2,1,0:T(8,128)(2,1)}), bf16[64,6,3584]{2,1,0:T(8,128)(2,1)}, u32[]{:S(2)}, u32[]{:S(2)}) async-start(bf16[64,6,3584]{2,1,0:T(8,128)(2,1)} %bitcast.84), calls=%async_computation.3 | async-start | bytes 7340032 | tf_op jit(solution)/shard_map/all_to_all | solution.py:77
  148.4 0.2 convolution_convert_fusion.4
  148.7 83.3 %all-to-all-done.3 = bf16[64,6,3584]{2,1,0:T(8,128)(2,1)} async-done(((bf16[64,6,3584]{2,1,0:T(8,128)(2,1)}), bf16[64,6,3584]{2,1,0:T(8,128)(2,1)}, u32[]{:S(2)}, u32[]{:S(2)}) %all-to-all-start.3) | async-done | bytes 2752544 | tf_op jit(solution)/shard_map/all_to_all | solution.py:77
  232.0 2.1 broadcast_in_dim.34
  234.1 7.4 %all-to-all-start.5 = ((bf16[64,6,3584]{2,1,0:T(8,128)(2,1)}), bf16[64,6,3584]{2,1,0:T(8,128)(2,1)}, u32[]{:S(2)}, u32[]{:S(2)}) async-start(bf16[64,6,3584]{2,1,0:T(8,128)(2,1)} %bitcast.83), calls=%async_computation.5 | async-start | bytes 7340032 | tf_op jit(solution)/shard_map/all_to_all | solution.py:78
  241.5 1.4 reshape.186
  242.9 1.8 copy.115
  245.1 79.2 %all-to-all-done.5 = bf16[64,6,3584]{2,1,0:T(8,128)(2,1)} async-done(((bf16[64,6,3584]{2,1,0:T(8,128)(2,1)}), bf16[64,6,3584]{2,1,0:T(8,128)(2,1)}, u32[]{:S(2)}, u32[]{:S(2)}) %all-to-all-start.5) | async-done | bytes 2752544 | tf_op jit(solution)/shard_map/all_to_all | solution.py:78
  324.3 1.0 stack.5
  325.3 7.9 %all-to-all-start.6 = ((bf16[8,1,448,128]{3,2,1,0:T(8,128)(2,1)}), bf16[8,1,448,128]{3,2,1,0:T(8,128)(2,1)}, u32[]{:S(2)}, u32[]{:S(2)}) async-start(bf16[8,1,448,128]{3,2,1,0:T(8,128)(2,1)} %stack.5), calls=%async_computation.6 | async-start | bytes 1835008 | tf_op jit(solution)/shard_map/all_to_all | solution.py:66
  333.5 1.4 reshape.182
  334.9 1.8 copy.109
  337.1 1.4 reshape.184
  338.5 1.8 copy.112
  340.7 28.9 %all_gather.6 = bf16[1,3584,128]{2,1,0:T(8,128)(2,1)S(1)} all-gather(bf16[1,448,128]{2,1,0:T(8,128)(2,1)S(1)} %copy.130), channel_id=1, replica_groups=mesh['dp'=8,'expert'=64] {'dp'}, dimensions={1}, use_global_device_ids=true | all-gather | bytes 1032192 | tf_op jit(solution)/shard_map/all_gather | solution.py:70
  369.5 16.6 %all_gather.7 = bf16[1,3584,128]{2,1,0:T(8,128)(2,1)S(1)} all-gather(bf16[1,448,128]{2,1,0:T(8,128)(2,1)S(1)} %copy.129), channel_id=1, replica_groups=mesh['dp'=8,'expert'=64] {'dp'}, dimensions={1}, use_global_device_ids=true | all-gather | bytes 1032192 | tf_op jit(solution)/shard_map/all_gather | solution.py:69
  386.1 5.4 reshape.160
  391.6 5.5 reshape.163
  397.1 2.9 fusion.9
  399.9 0.9 fusion.6
  400.9 3.7 fusion.12
  404.6 1.8 fusion.1
  406.4 3.3 fusion.4
  409.7 0.8 convert_element_type.149
  410.5 9.6 %all-to-all-start.8 = ((bf16[64,1,6]{2,1,0:T(2,128)(2,1)}), bf16[64,1,6]{2,1,0:T(2,128)(2,1)S(1)}, u32[]{:S(2)}, u32[]{:S(2)}) async-start(bf16[64,1,6]{2,1,0:T(2,128)(2,1)} %convert_element_type.149), calls=%async_computation.11 | async-start | bytes 65536 | tf_op jit(solution)/shard_map/all_to_all | solution.py:125
  420.1 5.0 fusion
  425.1 5.4 reshape.164
  430.6 10.8 %all-to-all-start.7 = ((bf16[64,6,3584]{2,1,0:T(8,128)(2,1)}), bf16[64,6,3584]{2,1,0:T(8,128)(2,1)}, u32[]{:S(2)}, u32[]{:S(2)}) async-start(bf16[64,6,3584]{2,1,0:T(8,128)(2,1)} %reshape.164), calls=%async_computation.10 | async-start | bytes 7340032 | tf_op jit(solution)/shard_map/all_to_all | solution.py:118
  441.4 3.7 fusion.2
  445.2 0.3 reduce-scatter.8.cloned.1.call-start
  445.4 3.7 fusion.3
  449.1 0.8 copy.131
  450.0 0.7 fusion.21
  450.8 1.6 convert_element_type.127
  452.4 44.4 %reduce-scatter.6.cloned.1.call-done = bf16[1,448,128]{2,1,0:T(8,128)(2,1)} async-done(((bf16[1,3584,128]{2,1,0:T(8,128)(2,1)}), bf16[1,448,128]{2,1,0:T(8,128)(2,1)}) %reduce-scatter.6.cloned.1.call-update) | async-done | bytes 114704 | tf_op jit(solution)/shard_map/reduce_scatter | solution.py:110
  496.8 1.6 convert_element_type.131
  498.4 41.5 %reduce-scatter.8.cloned.1.call-done = bf16[1,448,128]{2,1,0:T(8,128)(2,1)} async-done(((bf16[1,3584,128]{2,1,0:T(8,128)(2,1)}), bf16[1,448,128]{2,1,0:T(8,128)(2,1)}) %reduce-scatter.8.cloned.1.call-update) | async-done | bytes 114704 | tf_op jit(solution)/shard_map/reduce_scatter | solution.py:113
  540.0 1.6 convert_element_type.137
  541.6 2.8 convert_reduce_fusion
  544.4 1.8 convolution_convert_fusion
  (63 shorter events, 2.9 us)
Async XLA Ops:
  7.2 122.2 %copy-start = (bf16[128,3584]{1,0:T(8,128)(2,1)S(1)}, bf16[128,3584]{1,0:T(8,128)(2,1)}, u32[]{:S(2)}) copy-start(bf16[128,3584]{1,0:T(8,128)(2,1)} %param.7) | copy-start | bytes 2752516
  12.9 41.9 %all-to-all-start.4 = ((bf16[64,1,6]{2,1,0:T(2,128)(2,1)}), bf16[64,1,6]{2,1,0:T(2,128)(2,1)S(1)}, u32[]{:S(2)}, u32[]{:S(2)}) async-start(bf16[64,1,6]{2,1,0:T(2,128)(2,1)} %copy.122), calls=%async_computation.4 | async-start | bytes 65536 | tf_op jit(solution)/shard_map/all_to_all | solution.py:79
  27.2 35.4 %copy-start.6 = (bf16[1,3584,16]{1,2,0:T(8,128)(2,1)S(1)}, bf16[1,3584,16]{1,2,0:T(8,128)(2,1)}, u32[]{:S(2)}) copy-start(bf16[1,3584,16]{1,2,0:T(8,128)(2,1)} %param.12) | copy-start | bytes 344068
  54.8 33.6 %all-to-all-start = ((bf16[8,2,3584]{2,1,0:T(2,128)(2,1)}), bf16[8,2,3584]{2,1,0:T(2,128)(2,1)S(1)}, u32[]{:S(2)}, u32[]{:S(2)}) async-start(bf16[8,2,3584]{2,1,0:T(2,128)(2,1)} %reshape.181), calls=%async_computation | async-start | bytes 229376 | tf_op jit(solution)/shard_map/all_to_all | solution.py:57
  62.6 33.6 %copy-start.7 = (bf16[1,3584,16]{1,2,0:T(8,128)(2,1)S(1)}, bf16[1,3584,16]{1,2,0:T(8,128)(2,1)}, u32[]{:S(2)}) copy-start(bf16[1,3584,16]{1,2,0:T(8,128)(2,1)} %param.13) | copy-start | bytes 344068
  88.4 33.7 %all-to-all-start.1 = ((bf16[8,2,3584]{2,1,0:T(2,128)(2,1)}), bf16[8,2,3584]{2,1,0:T(2,128)(2,1)S(1)}, u32[]{:S(2)}, u32[]{:S(2)}) async-start(bf16[8,2,3584]{2,1,0:T(2,128)(2,1)} %reshape.183), calls=%async_computation.1 | async-start | bytes 229376 | tf_op jit(solution)/shard_map/all_to_all | solution.py:58
  122.1 12.8 %all-to-all-start.2 = ((bf16[8,2,3584]{2,1,0:T(2,128)(2,1)}), bf16[8,2,3584]{2,1,0:T(2,128)(2,1)S(1)}, u32[]{:S(2)}, u32[]{:S(2)}) async-start(bf16[8,2,3584]{2,1,0:T(2,128)(2,1)} %reshape.185), calls=%async_computation.2 | async-start | bytes 229376 | tf_op jit(solution)/shard_map/all_to_all | solution.py:59
  137.0 11.4 %copy-start.3 = (bf16[128,3584]{1,0:T(8,128)(2,1)S(1)}, bf16[128,3584]{1,0:T(8,128)(2,1)}, u32[]{:S(2)}) copy-start(bf16[128,3584]{1,0:T(8,128)(2,1)} %param.8) | copy-start | bytes 2752516
  137.0 95.0 %all-to-all-start.3 = ((bf16[64,6,3584]{2,1,0:T(8,128)(2,1)}), bf16[64,6,3584]{2,1,0:T(8,128)(2,1)}, u32[]{:S(2)}, u32[]{:S(2)}) async-start(bf16[64,6,3584]{2,1,0:T(8,128)(2,1)} %bitcast.84), calls=%async_computation.3 | async-start | bytes 7340032 | tf_op jit(solution)/shard_map/all_to_all | solution.py:77
  234.1 90.1 %all-to-all-start.5 = ((bf16[64,6,3584]{2,1,0:T(8,128)(2,1)}), bf16[64,6,3584]{2,1,0:T(8,128)(2,1)}, u32[]{:S(2)}, u32[]{:S(2)}) async-start(bf16[64,6,3584]{2,1,0:T(8,128)(2,1)} %bitcast.83), calls=%async_computation.5 | async-start | bytes 7340032 | tf_op jit(solution)/shard_map/all_to_all | solution.py:78
  325.3 75.5 %all-to-all-start.6 = ((bf16[8,1,448,128]{3,2,1,0:T(8,128)(2,1)}), bf16[8,1,448,128]{3,2,1,0:T(8,128)(2,1)}, u32[]{:S(2)}, u32[]{:S(2)}) async-start(bf16[8,1,448,128]{3,2,1,0:T(8,128)(2,1)} %stack.5), calls=%async_computation.6 | async-start | bytes 1835008 | tf_op jit(solution)/shard_map/all_to_all | solution.py:66
  333.3 117.5 %reduce-scatter.4.cloned.1.call-start = ((), (), s32[]{:S(2)}) async-start(), calls=%async_computation.12 | async-start | bytes 1032192 | tf_op jit(solution)/shard_map/reduce_scatter | solution.py:107
  337.1 32.4 %copy-start.4 = (bf16[1,448,128]{2,1,0:T(8,128)(2,1)}, bf16[1,448,128]{2,1,0:T(8,128)(2,1)S(1)}, u32[]{:S(2)}) copy-start(bf16[1,448,128]{2,1,0:T(8,128)(2,1)S(1)} %copy.129) | copy-start | bytes 344068
  340.7 50.9 %copy-start.5 = (bf16[1,448,128]{2,1,0:T(8,128)(2,1)}, bf16[1,448,128]{2,1,0:T(8,128)(2,1)S(1)}, u32[]{:S(2)}) copy-start(bf16[1,448,128]{2,1,0:T(8,128)(2,1)S(1)} %copy.130) | copy-start | bytes 344068
  397.1 2.9 copy-start.1
  400.9 3.7 copy-start.2
  410.5 20.0 %all-to-all-start.8 = ((bf16[64,1,6]{2,1,0:T(2,128)(2,1)}), bf16[64,1,6]{2,1,0:T(2,128)(2,1)S(1)}, u32[]{:S(2)}, u32[]{:S(2)}) async-start(bf16[64,1,6]{2,1,0:T(2,128)(2,1)} %convert_element_type.149), calls=%async_computation.11 | async-start | bytes 65536 | tf_op jit(solution)/shard_map/all_to_all | solution.py:125
  430.6 111.0 %all-to-all-start.7 = ((bf16[64,6,3584]{2,1,0:T(8,128)(2,1)}), bf16[64,6,3584]{2,1,0:T(8,128)(2,1)}, u32[]{:S(2)}, u32[]{:S(2)}) async-start(bf16[64,6,3584]{2,1,0:T(8,128)(2,1)} %reshape.164), calls=%async_computation.10 | async-start | bytes 7340032 | tf_op jit(solution)/shard_map/all_to_all | solution.py:118
  441.4 4.1 copy-start.8
  441.4 55.5 %reduce-scatter.6.cloned.1.call-start = ((), (), s32[]{:S(2)}) async-start(), calls=%async_computation.13 | async-start | bytes 1032192 | tf_op jit(solution)/shard_map/reduce_scatter | solution.py:110
  445.2 94.8 %reduce-scatter.8.cloned.1.call-start = ((), (), s32[]{:S(2)}) async-start(), calls=%async_computation.14 | async-start | bytes 1032192 | tf_op jit(solution)/shard_map/reduce_scatter | solution.py:113
Sparse Core Ops, SparseCore 0:
  409.9 40.5 reduce-scatter.3
  453.6 43.2 reduce-scatter.5
  499.7 40.2 reduce-scatter.7
